TPU v7x, 32 devices: a whole 2x2x4 slice. The times are simulated.
32 devices in a mesh: groups: 2 (over x), tensor: 16 (over z, y, core).
Axes of the slice: x: 2, y: 2, z: 4, core: 2. Of those that a mesh axis runs over, the one named last changes fastest.
Arguments:
- tokens: bfloat16 [64, 8192], P(('groups', 'tensor')), parts along dimension 0, may hold values from -6 to 6
- cotangent: bfloat16 [64, 8192], P(('groups', 'tensor')), parts along dimension 0, may hold values from -6 to 6
- up_blocks: bfloat16 [512, 128, 128], P('tensor'), may hold values from -0.1875 to 0.1875
- gate_blocks: bfloat16 [512, 128, 128], P('tensor'), may hold values from -0.1875 to 0.1875
- down_blocks: bfloat16 [512, 128, 128], P('tensor'), may hold values from -0.21875 to 0.21875
- up_layout: int32 [512], P('tensor'), may hold values from 0 to 191, as said below
- gate_layout: int32 [512], P('tensor'), may hold values from 0 to 191, as said below
- down_layout: int32 [512], P('tensor'), may hold values from 0 to 191, as said below
- live_counts: int32 [3, 16], P(None, 'tensor'), may hold values from 4 to 32, as said below
Outputs:
- output: bfloat16 [64, 8192], P(('groups', 'tensor')), parts along dimension 0
- grad_tokens: bfloat16 [64, 8192], P(('groups', 'tensor')), parts along dimension 0
- grad_up: bfloat16 [1024, 128, 128], P(('groups', 'tensor')), parts along dimension 0
- grad_gate: bfloat16 [1024, 128, 128], P(('groups', 'tensor')), parts along dimension 0
- grad_down: bfloat16 [1024, 128, 128], P(('groups', 'tensor')), parts along dimension 0
There are 2 independent parts, one for each index of `groups`. A program takes and returns all parts, laid end to end along the dimension named above; an argument that names none is the same for every part. Nothing has to cross between parts.
Inputs may be any that keep to these rules, and one draw needn't show every extreme that they name: `up_layout`: within the 32 slots of one owner the codes of one matrix are all different. `gate_layout`: within the 32 slots of one owner the codes of one matrix are all different. `down_layout`: within the 32 slots of one owner the codes of one matrix are all different. `live_counts`: in each of the three rows some owner has exactly 32 live slots; slots past an owner's count hold blocks that are not used.
All inputs are finite; a program needn't handle non-finite values.
Results may differ from a plain program's by a relative error of at most 0.0051.
Values may be sent and summed in bfloat16 or wider, within the bound.
A program may use at most 64 MiB of HBM per device.

v0:
```python
import jax
import jax.numpy as jnp
from jax import lax
from jax.sharding import PartitionSpec as P

HB_DEV = 3


def slot_tables(layout, count, major_size):
    slot_total = layout.shape[0]
    major = layout // HB_DEV
    minor = layout % HB_DEV
    live_mask = (jnp.arange(slot_total) < count).astype(jnp.float32)
    major_hot = (major[:, None] == jnp.arange(major_size)[None, :]).astype(jnp.float32)
    minor_hot = (minor[:, None] == jnp.arange(HB_DEV)[None, :]).astype(jnp.float32)
    return (major, minor, live_mask, major_hot, minor_hot)


def local(
    tokens,
    cotangent,
    up_blocks,
    gate_blocks,
    down_blocks,
    up_layout,
    gate_layout,
    down_layout,
    live_counts,
):
    highest = lax.Precision.HIGHEST
    f32 = jnp.float32
    x_full = lax.all_gather(tokens, "tensor", axis=0, tiled=True)
    dy_full = lax.all_gather(cotangent, "tensor", axis=0, tiled=True)
    row_total = x_full.shape[0]
    block_size = up_blocks.shape[1]
    width_blocks = x_full.shape[1] // block_size
    x_split = x_full.reshape(row_total, width_blocks, block_size)
    count_trio = live_counts[:, 0]
    up_major, up_minor, up_live, up_rowhot, up_hidhot = slot_tables(
        up_layout, count_trio[0], width_blocks
    )
    gate_major, gate_minor, gate_live, gate_rowhot, gate_hidhot = slot_tables(
        gate_layout, count_trio[1], width_blocks
    )
    down_major, down_minor, down_live, down_colhot, down_hidhot = slot_tables(
        down_layout, count_trio[2], width_blocks
    )
    w_up = up_blocks * up_live[:, None, None].astype(jnp.bfloat16)
    w_gate = gate_blocks * gate_live[:, None, None].astype(jnp.bfloat16)
    w_down = down_blocks * down_live[:, None, None].astype(jnp.bfloat16)
    x_up = jnp.take(x_split, up_major, axis=1)
    x_gate = jnp.take(x_split, gate_major, axis=1)
    up_terms = jnp.einsum("tsi,sij->tsj", x_up, w_up, preferred_element_type=f32)
    gate_terms = jnp.einsum("tsi,sij->tsj", x_gate, w_gate, preferred_element_type=f32)
    up_value = jnp.einsum("tsj,sh->thj", up_terms, up_hidhot, precision=highest)
    gate_value = jnp.einsum("tsj,sh->thj", gate_terms, gate_hidhot, precision=highest)
    sig = 1.0 / (1.0 + jnp.exp(-gate_value))
    act = gate_value * sig
    hidden = (act * up_value).astype(jnp.bfloat16)
    hid_down = jnp.take(hidden, down_minor, axis=1)
    out_terms = jnp.einsum("tsj,sjk->tsk", hid_down, w_down, preferred_element_type=f32)
    partial_out = jnp.einsum("tsk,sc->tck", out_terms, down_colhot, precision=highest).reshape(
        row_total, -1
    )
    out_share = lax.psum_scatter(partial_out, "tensor", scatter_dimension=0, tiled=True)
    dy_split = dy_full.reshape(row_total, width_blocks, block_size)
    dy_down = jnp.take(dy_split, down_major, axis=1)
    dh_terms = jnp.einsum("tsk,sjk->tsj", dy_down, w_down, preferred_element_type=f32)
    d_hidden = jnp.einsum("tsj,sh->thj", dh_terms, down_hidhot, precision=highest)
    d_up = (d_hidden * act).astype(jnp.bfloat16)
    d_gate = (d_hidden * up_value * sig * (1.0 + gate_value * (1.0 - sig))).astype(jnp.bfloat16)
    dup_slots = jnp.take(d_up, up_minor, axis=1)
    dgate_slots = jnp.take(d_gate, gate_minor, axis=1)
    dx_up = jnp.einsum("tsj,sij->tsi", dup_slots, w_up, preferred_element_type=f32)
    dx_gate = jnp.einsum("tsj,sij->tsi", dgate_slots, w_gate, preferred_element_type=f32)
    partial_dx = jnp.einsum("tsi,sr->tri", dx_up, up_rowhot, precision=highest)
    partial_dx = partial_dx + jnp.einsum("tsi,sr->tri", dx_gate, gate_rowhot, precision=highest)
    partial_dx = partial_dx.reshape(row_total, -1)
    dx_share = lax.psum_scatter(partial_dx, "tensor", scatter_dimension=0, tiled=True)
    grad_up = (
        jnp.einsum("tsi,tsj->sij", x_up, dup_slots, preferred_element_type=f32)
        * up_live[:, None, None]
    ).astype(jnp.bfloat16)
    grad_gate = (
        jnp.einsum("tsi,tsj->sij", x_gate, dgate_slots, preferred_element_type=f32)
        * gate_live[:, None, None]
    ).astype(jnp.bfloat16)
    grad_down = (
        jnp.einsum("tsj,tsk->sjk", hid_down, dy_down, preferred_element_type=f32)
        * down_live[:, None, None]
    ).astype(jnp.bfloat16)
    return (
        out_share.astype(jnp.bfloat16),
        dx_share.astype(jnp.bfloat16),
        grad_up,
        grad_gate,
        grad_down,
    )


def solution(mesh):
    placed = (
        P(("groups", "tensor"), None),
        P(("groups", "tensor"), None),
        P("tensor", None, None),
        P("tensor", None, None),
        P("tensor", None, None),
        P("tensor"),
        P("tensor"),
        P("tensor"),
        P(None, "tensor"),
    )
    return jax.shard_map(
        local,
        mesh=mesh,
        in_specs=placed,
        out_specs=(
            P(("groups", "tensor"), None),
            P(("groups", "tensor"), None),
            P(("groups", "tensor"), None, None),
            P(("groups", "tensor"), None, None),
            P(("groups", "tensor"), None, None),
        ),
        check_vma=False,
    )
```

profile of v0, /device:TPU:0, one launch (start us, length us, event | category | flops | bytes accessed | tf_op | source)
XLA Modules:
  0.0 150.8 jit_solution(14236068998945516922)
XLA Ops:
  0.6 0.7 compare_and_fusion.1
  1.3 24.8 %all-gather = bf16[16,2,8192]{2,1,0:T(2,128)(2,1)S(1)} all-gather(bf16[1,2,8192]{2,1,0:T(2,128)(2,1)} %bitcast.118), channel_id=1, replica_groups=mesh['groups'=2,'tensor'=16] {'tensor'}, dimensions={0}, use_global_device_ids=true | all-gather | bytes 557056 | tf_op jit(solution)/shard_map/all_gather | solution.py:32
  26.1 0.4 reshape.71
  26.5 0.0 copy-start.4
  26.5 0.0 copy-start
  26.5 0.3 copy.44
  26.9 0.6 gather_fusion.1
  27.5 0.0 copy-done.4
  27.5 0.6 fusion.74
  28.1 0.6 fusion.73
  28.8 0.0 copy-done
  28.8 0.0 copy-start.5
  28.8 0.5 convolution_bitcast_fusion.1
  29.3 0.6 fusion.13
  29.8 0.0 copy-done.5
  29.9 0.6 gather_fusion
  30.5 0.6 fusion.72
  31.2 0.0 copy-start.6
  31.2 0.0 copy-start.3
  31.2 1.7 %convolution_bitcast_fusion.2 = f32[32,32,128]{2,0,1:T(8,128)S(1)} fusion(bf16[32,128,128]{2,1,0:T(8,128)(2,1)} %param.16, bf16[32]{0:T(256)(128)(2,1)S(1)} %fusion.72, bf16[32,32,128]{2,1,0:T(8,128)(2,1)S(1)} %gather_fusion, pred[32]{0:T(512)(128)(4,1)S(1)} %get-tuple-element.26), kind=kOutput, calls=%fused_computation.12 | convolution fusion | flops 35782656 | bytes 1835104 | tf_op jit(solution)/shard_map/tsi,sij->tsj/dot_general | solution.py:54
  32.9 0.6 fusion.15
  33.5 0.0 copy-done.6
  33.5 0.0 copy-done.3
  33.5 18.9 %all-gather.1 = bf16[16,2,8192]{2,1,0:T(2,128)(2,1)S(1)} all-gather(bf16[1,2,8192]{2,1,0:T(2,128)(2,1)S(1)} %bitcast.119), channel_id=1, replica_groups=mesh['groups'=2,'tensor'=16] {'tensor'}, dimensions={0}, use_global_device_ids=true | all-gather | bytes 557056 | tf_op jit(solution)/shard_map/all_gather | solution.py:33
  52.4 0.4 reshape.73
  52.8 0.3 copy.51
  53.2 0.6 gather_fusion.3
  53.8 0.6 fusion.71
  54.3 1.9 %convolution_bitcast_fusion.5 = f32[32,32,128]{2,0,1:T(8,128)S(1)} fusion(bf16[32,128,128]{2,1,0:T(8,128)(2,1)} %param.17, bf16[32]{0:T(256)(128)(2,1)S(1)} %fusion.71, bf16[32,32,128]{2,1,0:T(8,128)(2,1)S(1)} %gather_fusion.3, pred[32]{0:T(512)(128)(4,1)S(1)} %get-tuple-element.13), kind=kOutput, calls=%fused_computation.15 | convolution fusion | flops 34209792 | bytes 1835104 | tf_op jit(solution)/shard_map/tsk,sjk->tsj/dot_general | solution.py:68
  56.3 0.6 fusion.9
  57.0 0.6 gather_fusion.4
  57.6 0.7 convolution_bitcast_fusion.4
  58.3 0.0 copy-start.1
  58.3 0.9 fusion.7
  59.3 1.3 gather_fusion.5
  60.6 0.0 copy-done.1
  60.6 1.7 %convolution_bitcast_fusion.3 = f32[32,32,128]{2,0,1:T(8,128)S(1)} fusion(bf16[32,128,128]{2,1,0:T(8,128)(2,1)S(1)} %copy-done.1, bf16[32]{0:T(256)(128)(2,1)S(1)} %fusion.72, bf16[32,32,128]{2,1,0:T(8,128)(2,1)} %gather_fusion.5, pred[32]{0:T(512)(128)(4,1)S(1)} %get-tuple-element.9), kind=kOutput, calls=%fused_computation.13 | convolution fusion | flops 34209792 | bytes 1835104 | tf_op jit(solution)/shard_map/tsj,sij->tsi/dot_general | solution.py:75
  62.2 1.0 convolution_add_fusion
  63.2 0.0 copy-start.2
  63.2 0.6 copy.82
  63.9 0.6 gather_fusion.2
  64.5 0.0 copy-done.2
  64.5 0.5 convolution_bitcast_fusion
  65.0 0.9 fusion.11
  65.9 0.6 copy.83
  66.5 0.0 copy-start.7
  66.5 73.7 %all-reduce.4 = (bf16[32,8192]{1,0:T(8,128)(2,1)}, bf16[32,8192]{1,0:T(8,128)(2,1)}) all-reduce(f32[32,8192]{1,0:T(8,128)S(1)} %bitcast.115, f32[32,8192]{1,0:T(8,128)S(1)} %bitcast.114), channel_id=2, replica_groups=mesh['groups'=2,'tensor'=16] {'tensor'}, use_global_device_ids=true, to_apply=%region_0.3.clone | all-reduce | flops 524288 | bytes 3145728
  140.2 0.0 copy-done.7
  140.2 0.6 dynamic-slice
  141.4 1.7 %dynamic-slice_convert_fusion = (bf16[2,8192]{1,0:T(2,128)(2,1)}, bf16[2,8192]{1,0:T(2,128)(2,1)}) fusion(bf16[32,8192]{1,0:T(8,128)(2,1)} %get-tuple-element.8, u32[]{:T(128)S(6)} %multiply.1, bf16[32,8192]{1,0:T(8,128)(2,1)} %get-tuple-element.7), kind=kLoop, calls=%fused_computation.59 | loop fusion | bytes 131076 | tf_op jit(solution)/shard_map/convert_element_type | solution.py:94
  143.1 0.6 compare_convert_fusion.1
  143.8 2.6 %multiply_convert_fusion.1 = bf16[32,128,128]{2,1,0:T(8,128)(2,1)} fusion(f32[32]{0:T(128)S(1)} %compare_convert_fusion.1, bf16[32,32,128]{2,1,0:T(8,128)(2,1)S(1)} %gather_fusion, pred[32]{0:T(512)(128)(4,1)S(1)} %get-tuple-element.26, bf16[32,32,128]{2,1,0:T(8,128)(2,1)} %gather_fusion.5, pred[32]{0:T(512)(128)(4,1)S(1)} %get-tuple-element.9), kind=kOutput, calls=%fused_computation.7 | convolution fusion | flops 34865152 | bytes 1573056 | tf_op jit(solution)/shard_map/tsi,tsj->sij/dot_general | solution.py:85
  146.3 0.6 compare_convert_fusion
  147.0 1.6 %multiply_convert_fusion.2 = bf16[32,128,128]{2,1,0:T(8,128)(2,1)} fusion(f32[32]{0:T(128)S(1)} %compare_convert_fusion, bf16[32,32,128]{2,1,0:T(8,128)(2,1)S(1)} %gather_fusion.1, pred[32]{0:T(512)(128)(4,1)S(1)} %get-tuple-element.31, bf16[32,32,128]{2,1,0:T(8,128)(2,1)S(1)} %gather_fusion.4, pred[32]{0:T(512)(128)(4,1)S(1)} %get-tuple-element.11), kind=kOutput, calls=%fused_computation.8 | convolution fusion | flops 34865152 | bytes 1573056 | tf_op jit(solution)/shard_map/tsi,tsj->sij/dot_general | solution.py:81
  148.6 0.6 compare_convert_fusion.2
  149.2 1.6 %multiply_convert_fusion = bf16[32,128,128]{2,1,0:T(8,128)(2,1)} fusion(f32[32]{0:T(128)S(1)} %compare_convert_fusion.2, bf16[32,32,128]{2,1,0:T(8,128)(2,1)S(1)} %gather_fusion.2, pred[32]{0:T(512)(128)(4,1)S(1)} %get-tuple-element.24, bf16[32,32,128]{2,1,0:T(8,128)(2,1)S(1)} %gather_fusion.3, pred[32]{0:T(512)(128)(4,1)S(1)} %get-tuple-element.13), kind=kOutput, calls=%fused_computation.6 | convolution fusion | flops 34865152 | bytes 1573056 | tf_op jit(solution)/shard_map/tsj,tsk->sjk/dot_general | solution.py:89
  (15 shorter events, 0.1 us)
Async XLA Ops:
  26.5 1.0 copy-start.4
  26.5 2.2 %copy-start = (bf16[32,128,128]{2,1,0:T(8,128)(2,1)S(1)}, bf16[32,128,128]{2,1,0:T(8,128)(2,1)}, u32[]{:S(2)}) copy-start(bf16[32,128,128]{2,1,0:T(8,128)(2,1)} %param.15) | copy-start | bytes 3145732
  28.8 1.1 copy-start.5
  31.2 2.3 %copy-start.6 = (s32[32]{0:T(128)S(1)}, s32[32]{0:T(128)}, u32[]{:S(2)}) copy-start(s32[32]{0:T(128)} %param.20) | copy-start | bytes 388
  31.2 2.4 %copy-start.3 = (bf16[2,8192]{1,0:T(2,128)(2,1)S(1)}, bf16[2,8192]{1,0:T(2,128)(2,1)}, u32[]{:S(2)}) copy-start(bf16[2,8192]{1,0:T(2,128)(2,1)} %param.14) | copy-start | bytes 98308
  58.3 2.3 %copy-start.1 = (bf16[32,128,128]{2,1,0:T(8,128)(2,1)S(1)}, bf16[32,128,128]{2,1,0:T(8,128)(2,1)}, u32[]{:S(2)}) copy-start(bf16[32,128,128]{2,1,0:T(8,128)(2,1)} %param.16) | copy-start | bytes 3145732
  63.2 1.3 copy-start.2
  66.5 73.7 %copy-start.7 = (u32[32]{0:T(128)S(1)}, u32[32]{0:T(128)}, u32[]{:S(2)}) copy-start(u32[32]{0:T(128)} %constant.59) | copy-start | bytes 388
where the time goes:
time: 151 us
  blocking collectives  117 us (77%)
  matrix products  17.4 us (12%)
  local copies, waits for them, and re-layouts  9.91 us (7%)
  other arithmetic  4.48 us (3%)
  between operations  1.64 us (1%)
    unnamed x1, blocking collectives  73.7 us
    all_gather x1, blocking collectives, local(): x_full = lax.all_gather(tokens, 'tensor', axis=0, tiled=True)  24.8 us
    all_gather x1, blocking collectives, local(): dy_full = lax.all_gather(cotangent, 'tensor', axis=0, tiled=True)  18.9 us

commit v1 on v0

v1 whole, which is shorter than its diff:
```python
import functools

import jax
import jax.numpy as jnp
from jax import lax
from jax.experimental import pallas as pl
from jax.experimental.pallas import tpu as pltpu
from jax.sharding import PartitionSpec as P

HB = 3
BF16 = jnp.bfloat16
F32 = jnp.float32
NT = (((1,), (1,)), ((), ()))
TN = (((0,), (0,)), ((), ()))


def third(code):
    return (code * 171) >> 9


def layer_kernel(
    n, lay_ref, cnt_ref, tok_ref, cot_ref, wu_hbm, wg_hbm, wd_hbm,
    xg, yg, hid, dup, dgt, outp, dxp,
    wu, wg, wd, mx, terms, terms2, inv_v, inv_s, po, own, r1, t2, r2, t3, r3,
    wsem, isem, gsend, grecv, s1, q1, lsem, s2, q2, s3, q3,
):
    nz = n // 4
    db = xg.shape[0]
    rows = xg.shape[2]
    bs = xg.shape[3]
    tt = n * rows
    slots = wu.shape[0]
    me = lax.axis_index("tensor")
    z, y, p = me // 4, (me // 2) % 2, me % 2
    sib = me + 1 - 2 * p
    pair = me + 2 - 4 * y
    zs = [(z + k) % nz for k in range(nz)]

    def at(zz, yy, pp):
        return zz * 4 + yy * 2 + pp

    def dev(j):
        return {"tensor": j}

    wcopies = [
        pltpu.make_async_copy(src, dst, wsem.at[i])
        for i, (src, dst) in enumerate(((wu_hbm, wu), (wg_hbm, wg), (wd_hbm, wd)))
    ]
    for c in wcopies:
        c.start()

    barrier = pltpu.get_barrier_semaphore()
    for j in [at(zz, y, p) for zz in zs[1:]] + [pair, sib]:
        pl.semaphore_signal(
            barrier, inc=1, device_id=dev(j), device_id_type=pl.DeviceIdType.MESH
        )

    for c in range(db):
        xg[c, me] = tok_ref[:, c * bs:(c + 1) * bs]
        yg[c, me] = cot_ref[:, c * bs:(c + 1) * bs]

    pl.semaphore_wait(barrier, nz - 1 + 2)

    gbuf = (xg, yg)
    nsend = [0, 0]
    pending = []

    def gsendto(a, chunk, j):
        c = pltpu.make_async_remote_copy(
            src_ref=gbuf[a].at[:, chunk],
            dst_ref=gbuf[a].at[:, chunk],
            send_sem=gsend.at[a, nsend[a]],
            recv_sem=grecv.at[a, chunk],
            device_id=dev(j),
            device_id_type=pl.DeviceIdType.MESH,
        )
        nsend[a] += 1
        c.start()
        pending.append(c)

    def gwait(a, chunk):
        pltpu.make_async_remote_copy(
            src_ref=gbuf[a].at[:, chunk],
            dst_ref=gbuf[a].at[:, chunk],
            send_sem=gsend.at[a, 0],
            recv_sem=grecv.at[a, chunk],
            device_id=dev(sib),
            device_id_type=pl.DeviceIdType.MESH,
        ).wait_recv()

    for a in range(2):
        for zz in zs[1:]:
            gsendto(a, me, at(zz, y, p))
        gsendto(a, me, pair)
        gsendto(a, me, sib)

    lane = lax.broadcasted_iota(jnp.int32, (8, 256), 1)
    for m in range(3):
        tab = jnp.full((8, 256), slots, jnp.int32)
        for s in range(slots):
            code = jnp.where(s < cnt_ref[m, 0], lay_ref[m, s], -1)
            tab = jnp.where(lane == code, s, tab)
        inv_v[m] = tab
    icopy = pltpu.make_async_copy(inv_v, inv_s, isem.at[0])
    icopy.start()
    terms[slots] = jnp.zeros((tt, bs), F32)
    terms2[slots] = jnp.zeros((tt, bs), F32)

    def forward_z(a):
        for zz in zs[1:]:
            gwait(a, at(zz, y, p))
            gsendto(a, at(zz, y, p), pair)
            gsendto(a, at(zz, y, p), sib)

    def forward_y(a):
        for zz in zs:
            gwait(a, at(zz, 1 - y, p))
            gsendto(a, at(zz, 1 - y, p), sib)

    def finish(a):
        for zz in zs:
            gwait(a, at(zz, y, 1 - p))
            gwait(a, at(zz, 1 - y, 1 - p))

    def contract(src, m, weights, transposed):
        view = src.reshape(db, tt, bs)

        def pick(s, carry):
            code = lay_ref[m, s]
            major = third(code)
            minor = jnp.where(s < cnt_ref[m, 0], code - 3 * major, HB)
            rows_s = view[major]
            for h in range(HB):
                mx[s, h * tt:(h + 1) * tt, :] = jnp.where(
                    minor == h, rows_s, jnp.zeros_like(rows_s)
                )
            return carry

        lax.fori_loop(0, slots, pick, 0, unroll=True)
        acc = jnp.zeros((HB * tt, bs), F32)
        for s in range(slots):
            if transposed:
                acc += lax.dot_general(mx[s], weights[s], NT, preferred_element_type=F32)
            else:
                acc += jnp.dot(mx[s], weights[s], preferred_element_type=F32)
        return acc

    def scatter(a, tables):
        pov = po.at[a].reshape(db, tt, bs)

        def place(c, carry):
            total = jnp.zeros((tt, bs), F32)
            for m, source in tables:
                for h in range(HB):
                    total += source[inv_s[m, 0, c * HB + h]]
            pov[c] = total.astype(BF16)
            return carry

        lax.fori_loop(0, db, place, 0, unroll=4)

    flat = (db * rows, bs)
    order = zs[1:] + zs[:1]

    def remote(src, dst, send, recv, j):
        return pltpu.make_async_remote_copy(
            src_ref=src, dst_ref=dst, send_sem=send, recv_sem=recv,
            device_id=dev(j), device_id_type=pl.DeviceIdType.MESH,
        )

    def copy1(a, zz, yy):
        return remote(
            po.at[a, :, at(zz, yy, 1 - p)], r1.at[a, zz, yy],
            s1.at[a, zz, yy], q1.at[a, zz, yy], sib,
        )

    def local(a, zz, yy):
        return pltpu.make_async_copy(
            po.at[a, :, at(zz, yy, p)], own.at[a, zz, yy], lsem.at[a, zz, yy]
        )

    def copy2(a, zz):
        return remote(t2.at[a, zz], r2.at[a, zz], s2.at[a, zz], q2.at[a, zz], pair)

    def copy3(a, zz, slot):
        return remote(
            t3.at[a, zz], r3.at[a, slot], s3.at[a, zz], q3.at[a, slot], at(zz, y, p)
        )

    def reduce_core(a):
        for yy in (1 - y, y):
            for zz in order:
                copy1(a, zz, yy).start()
                local(a, zz, yy).start()

    def load(ref, *idx):
        return ref.at[idx].reshape(*flat)[...].astype(F32)

    def store(ref, value, *idx):
        ref.at[idx].reshape(*flat)[...] = value.astype(BF16)

    def reduce_pair(a):
        for zz in order:
            copy1(a, zz, 1 - y).wait_recv()
            local(a, zz, 1 - y).wait()
            store(t2, load(own, a, zz, 1 - y) + load(r1, a, zz, 1 - y), a, zz)
            copy2(a, zz).start()

    def reduce_z(a):
        for zz in order:
            copy1(a, zz, y).wait_recv()
            local(a, zz, y).wait()
            copy2(a, zz).wait_recv()
            total = load(own, a, zz, y) + load(r1, a, zz, y) + load(r2, a, zz)
            if zz is zs[0]:
                return total
            store(t3, total, a, zz)
            copy3(a, zz, z).start()

    def reduce_end(a, total, result):
        for zz in zs[1:]:
            copy3(a, zz, zz).wait_recv()
            total += load(r3, a, zz)
        result.reshape(*flat)[...] = total.astype(BF16)
        for zz in order:
            for yy in (0, 1):
                copy1(a, zz, yy).wait_send()
            copy2(a, zz).wait_send()
        for zz in zs[1:]:
            copy3(a, zz, z).wait_send()

    def expand(weights, src, m, dst, dims):
        for s in range(slots):
            minor = lay_ref[m, s] - 3 * third(lay_ref[m, s])
            dst[s] = lax.dot_general(
                src[minor], weights[s], dims, preferred_element_type=F32
            )

    forward_z(0)
    forward_y(0)
    forward_z(1)
    finish(0)
    wcopies[0].wait()
    up = contract(xg, 0, wu, False)
    wcopies[1].wait()
    gate = contract(xg, 1, wg, False)
    sig = 1.0 / (1.0 + jnp.exp(-gate))
    act = gate * sig
    hid.reshape(HB * tt, bs)[...] = (act * up).astype(BF16)
    forward_y(1)
    wcopies[2].wait()
    icopy.wait()
    expand(wd, hid, 2, terms, (((1,), (0,)), ((), ())))
    scatter(0, ((2, terms),))
    reduce_core(0)
    finish(1)
    d_hidden = contract(yg, 2, wd, True)
    dup.reshape(HB * tt, bs)[...] = (d_hidden * act).astype(BF16)
    dgt.reshape(HB * tt, bs)[...] = (
        d_hidden * up * sig * (1.0 + gate * (1.0 - sig))
    ).astype(BF16)
    reduce_pair(0)
    expand(wu, dup, 0, terms, NT)
    expand(wg, dgt, 1, terms2, NT)
    scatter(1, ((0, terms), (1, terms2)))
    reduce_core(1)
    total0 = reduce_z(0)
    reduce_pair(1)
    total1 = reduce_z(1)
    reduce_end(0, total0, outp)
    reduce_end(1, total1, dxp)
    for c in pending:
        c.wait_send()


def grads_kernel(
    per, lay_ref, cnt_ref, xg, yg, hid, dup, dgt, outp, dxp,
    out, dx, gu, gg, gd,
):
    step = pl.program_id(0)
    db, _, bs = outp.shape

    @pl.when(step == 0)
    def _():
        for c in range(db):
            out[:, c * bs:(c + 1) * bs] = outp[c]
            dx[:, c * bs:(c + 1) * bs] = dxp[c]

    for i in range(per):
        s = step * per + i
        for m, grad in ((0, gu), (1, gg), (2, gd)):
            code = lay_ref[m, s]
            major = third(code)
            minor = code - 3 * major
            if m == 2:
                lhs, rhs = hid[minor], yg[major]
            else:
                lhs, rhs = xg[major], (dup, dgt)[m][minor]
            lhs = jnp.where(s < cnt_ref[m, 0], lhs, jnp.zeros_like(lhs))
            grad[i] = lax.dot_general(
                lhs, rhs, TN, preferred_element_type=F32
            ).astype(BF16)


def local_part(n, tokens, cotangent, wu, wg, wd, lu, lg, ld, counts):
    rows, width = tokens.shape
    slots, bs, _ = wu.shape
    db, tt, nz = width // bs, n * rows, n // 4
    layout = jnp.stack([lu, lg, ld])
    vm = pl.BlockSpec(memory_space=pltpu.VMEM)
    sm = pl.BlockSpec(memory_space=pltpu.SMEM)
    hbm = pl.BlockSpec(memory_space=pl.ANY)
    shape = jax.ShapeDtypeStruct
    dma = pltpu.SemaphoreType.DMA
    part = (nz, db, rows, bs)
    xg, yg, hid, dup, dgt, outp, dxp = pl.pallas_call(
        functools.partial(layer_kernel, n),
        out_shape=[shape((db, n, rows, bs), BF16)] * 2
        + [shape((HB, tt, bs), BF16)] * 3
        + [shape((db, rows, bs), BF16)] * 2,
        in_specs=[sm, sm, vm, vm, hbm, hbm, hbm],
        out_specs=[vm] * 7,
        scratch_shapes=[
            pltpu.VMEM((slots, bs, bs), BF16),
            pltpu.VMEM((slots, bs, bs), BF16),
            pltpu.VMEM((slots, bs, bs), BF16),
            pltpu.VMEM((slots, HB * tt, bs), BF16),
            pltpu.VMEM((slots + 1, tt, bs), F32),
            pltpu.VMEM((slots + 1, tt, bs), F32),
            pltpu.VMEM((3, 8, 256), jnp.int32),
            pltpu.SMEM((3, 8, 256), jnp.int32),
            pltpu.VMEM((2, db, n, rows, bs), BF16),
            pltpu.VMEM((2, nz, 2, db, rows, bs), BF16),
            pltpu.VMEM((2, nz, 2, db, rows, bs), BF16),
            pltpu.VMEM((2,) + part, BF16),
            pltpu.VMEM((2,) + part, BF16),
            pltpu.VMEM((2,) + part, BF16),
            pltpu.VMEM((2,) + part, BF16),
            dma((3,)), dma((1,)), dma((2, n)), dma((2, n)),
            dma((2, nz, 2)), dma((2, nz, 2)), dma((2, nz, 2)),
            dma((2, nz)), dma((2, nz)), dma((2, nz)), dma((2, nz)),
        ],
        compiler_params=pltpu.CompilerParams(
            collective_id=0, has_side_effects=True, vmem_limit_bytes=48 << 20
        ),
        name="layer",
    )(layout, counts, tokens, cotangent, wu, wg, wd)
    xg = xg.reshape(db, tt, bs)
    yg = yg.reshape(db, tt, bs)
    per = slots // 4
    block = pl.BlockSpec((per, bs, bs), lambda i: (i, 0, 0))
    row = pl.BlockSpec((rows, width), lambda i: (0, 0))

    def whole(a):
        return pl.BlockSpec(a.shape, lambda i: (0,) * a.ndim)

    rest = (xg, yg, hid, dup, dgt, outp, dxp)
    return pl.pallas_call(
        functools.partial(grads_kernel, per),
        grid=(4,),
        out_shape=[shape((rows, width), BF16)] * 2 + [shape((slots, bs, bs), BF16)] * 3,
        in_specs=[sm, sm] + [whole(a) for a in rest],
        out_specs=[row, row, block, block, block],
        compiler_params=pltpu.CompilerParams(vmem_limit_bytes=48 << 20),
        name="grads",
    )(layout, counts, *rest)


def solution(mesh):
    n = mesh.shape["tensor"]
    both = ("groups", "tensor")
    return jax.shard_map(
        functools.partial(local_part, n),
        mesh=mesh,
        in_specs=(
            P(both, None), P(both, None),
            P("tensor", None, None), P("tensor", None, None), P("tensor", None, None),
            P("tensor"), P("tensor"), P("tensor"), P(None, "tensor"),
        ),
        out_specs=(
            P(both, None), P(both, None),
            P(both, None, None), P(both, None, None), P(both, None, None),
        ),
        check_vma=False,
    )
```

time: 151 us -> 46.8 us (0.31)
  blocking collectives: 117 us -> 0 us
  Pallas kernels: 0 us -> 39.1 us
  matrix products: 17.4 us -> 0 us
  other arithmetic: 4.48 us -> 0.01 us
  local copies, waits for them, and re-layouts: 9.91 us -> 6.59 us
    unnamed x1 -> x0, blocking collectives: 73.7 us -> none
    all_gather x2 -> x0, blocking collectives: 43.7 us -> none  [the longest x1 24.8 us: local(): x_full = lax.all_gather(tokens, 'tensor', axis=0, tiled=True)]
    pallas_call x0 -> x2, Pallas kernels: none -> 39.1 us  [the longest x1 35.5 us: local_part(): pl.pallas_call(functools.partial(layer_kernel, n), out_shape=[shape((db,...]
    dot_general x15 -> x0, matrix products: 17.4 us -> none  [the longest x1 2.58 us: local(): jnp.einsum('tsi,tsj->sij', x_gate, dgate_slots, preferred_element_type=f32)]
    unnamed x19, local copies, waits for them, and re-layouts: 1.85 us -> 6.59 us
    gather x6 -> x0, local copies, waits for them, and re-layouts: 4.3 us -> none  [the longest x1 1.29 us: local(): dgate_slots = jnp.take(d_gate, gate_minor, axis=1)]
    convert_element_type x7 -> x0, other arithmetic: 3.71 us -> none  [the longest x3 1.83 us: slot_tables(): live_mask = (jnp.arange(slot_total) < count).astype(jnp.float32)]
    convert_element_type x1 -> x0, local copies, waits for them, and re-layouts: 1.67 us -> none  [local(): dx_share.astype(jnp.bfloat16)]
where the time goes in v1:
time: 46.8 us; the launch traced here: 46.4 us
  Pallas kernels  39.1 us (84%)
  local copies, waits for them, and re-layouts  6.59 us (14%)
  between operations  0.67 us (1%)
    pallas_call x1, Pallas kernels, local_part(): pl.pallas_call(functools.partial(layer_kernel, n), out_shape=[shape((db,...  35.5 us
    unnamed x19, local copies, waits for them, and re-layouts  6.59 us
    pallas_call x1, Pallas kernels, local_part(): pl.pallas_call(functools.partial(grads_kernel, per), grid=(4,), out_shape...  3.63 us

profile of v1, /device:TPU:0, one launch (start us, length us, event | category | flops | bytes accessed | tf_op | source)
XLA Modules:
  0.0 46.4 jit_solution(17458594239822814346)
XLA Ops:
  0.6 0.0 copy-start.5
  0.6 0.0 copy-start.6
  0.7 0.0 copy-start.7
  0.7 0.6 %copy-done.5 = s32[32]{0:T(128)S(1)} copy-done((s32[32]{0:T(128)S(1)}, s32[32]{0:T(128)}, u32[]{:S(2)}) %copy-start.5) | copy-done | bytes 152
  1.3 0.0 copy-done.6
  1.3 0.0 copy-done.7
  1.3 0.0 copy-start.8
  1.3 0.6 %copy-done.8 = s32[3,1]{0,1:T(1,128)S(1)} copy-done((s32[3,1]{0,1:T(1,128)S(1)}, s32[3,1]{0,1:T(1,128)}, u32[]{:S(2)}) %copy-start.8) | copy-done | bytes 36
  2.0 0.1 copy.15.cnt_ref
  2.1 0.0 copy-start
  2.1 1.2 %copy-done = bf16[32,128,128]{2,1,0:T(8,128)(2,1)S(1)} copy-done((bf16[32,128,128]{2,1,0:T(8,128)(2,1)S(1)}, bf16[32,128,128]{2,1,0:T(8,128)(2,1)}, u32[]{:S(2)}) %copy-start) | copy-done | bytes 1048600
  3.3 0.0 copy-start.1
  3.3 1.2 %copy-done.1 = bf16[32,128,128]{2,1,0:T(8,128)(2,1)S(1)} copy-done((bf16[32,128,128]{2,1,0:T(8,128)(2,1)S(1)}, bf16[32,128,128]{2,1,0:T(8,128)(2,1)}, u32[]{:S(2)}) %copy-start.1) | copy-done | bytes 1048600
  4.5 0.0 copy-start.2
  4.5 1.2 %copy-done.2 = bf16[32,128,128]{2,1,0:T(8,128)(2,1)S(1)} copy-done((bf16[32,128,128]{2,1,0:T(8,128)(2,1)S(1)}, bf16[32,128,128]{2,1,0:T(8,128)(2,1)}, u32[]{:S(2)}) %copy-start.2) | copy-done | bytes 1048600
  5.7 0.0 copy-start.3
  5.7 0.8 %copy-done.3 = bf16[2,8192]{1,0:T(2,128)(2,1)S(1)} copy-done((bf16[2,8192]{1,0:T(2,128)(2,1)S(1)}, bf16[2,8192]{1,0:T(2,128)(2,1)}, u32[]{:S(2)}) %copy-start.3) | copy-done | bytes 32792
  6.5 0.0 copy-start.4
  6.5 0.8 %copy-done.4 = bf16[2,8192]{1,0:T(2,128)(2,1)S(1)} copy-done((bf16[2,8192]{1,0:T(2,128)(2,1)S(1)}, bf16[2,8192]{1,0:T(2,128)(2,1)}, u32[]{:S(2)}) %copy-start.4) | copy-done | bytes 32792
  7.3 35.5 %layer.1 = (bf16[64,16,2,128]{3,2,1,0:T(2,128)(2,1)S(1)}, bf16[64,16,2,128]{3,2,1,0:T(2,128)(2,1)S(1)}, bf16[3,32,128]{2,1,0:T(8,128)(2,1)S(1)}, bf16[3,32,128]{...) custom-call(s32[3,32]{1,0:T(4,128)S(1)} %pad_add_fusion.lay_ref, ...), custom_call_target="tpu_custom_call" | custom-call | tf_op jit(solution)/shard_map/layer/pallas_call | solution.py:315
  42.7 3.6 %grads.1 = (bf16[2,8192]{1,0:T(2,128)(2,1)}, bf16[2,8192]{1,0:T(2,128)(2,1)}, bf16[32,128,128]{2,1,0:T(8,128)(2,1)}, bf16[32,128,128]{2,1,0:T(8,128)(2,1)}, bf16[32,128,128]{2,1,0:T(8,128)(2,1)}) custom-call(s32[3,32]{1,0:T(4,128)S(1)} %pad_add_fusion.lay_ref, s32[3,1]{1,0:T(4,128)S(1)} %copy.15.cnt_ref, bf16[64,32,128]{2,1,0:T(8,128)(2,1)S(1)} %bitcast.5, ...), custom_call_target="tpu_custom_call" | custom-call | tf_op jit(solution)/shard_map/grads/pallas_call | solution.py:357
  (1 shorter events, 0.0 us)
Async XLA Ops:
  0.6 0.7 %copy-start.5 = (s32[32]{0:T(128)S(1)}, s32[32]{0:T(128)}, u32[]{:S(2)}) copy-start(s32[32]{0:T(128)} %param.16) | copy-start | bytes 388
  0.6 0.7 %copy-start.6 = (s32[32]{0:T(128)S(1)}, s32[32]{0:T(128)}, u32[]{:S(2)}) copy-start(s32[32]{0:T(128)} %param.15) | copy-start | bytes 388
  0.7 0.7 %copy-start.7 = (s32[32]{0:T(128)S(1)}, s32[32]{0:T(128)}, u32[]{:S(2)}) copy-start(s32[32]{0:T(128)} %param.14) | copy-start | bytes 388
  1.3 0.7 %copy-start.8 = (s32[3,1]{0,1:T(1,128)S(1)}, s32[3,1]{0,1:T(1,128)}, u32[]{:S(2)}) copy-start(s32[3,1]{0,1:T(1,128)} %param.17) | copy-start | bytes 40
  2.1 1.2 %copy-start = (bf16[32,128,128]{2,1,0:T(8,128)(2,1)S(1)}, bf16[32,128,128]{2,1,0:T(8,128)(2,1)}, u32[]{:S(2)}) copy-start(bf16[32,128,128]{2,1,0:T(8,128)(2,1)} %wu_hbm.1) | copy-start | bytes 3145732
  3.3 1.2 %copy-start.1 = (bf16[32,128,128]{2,1,0:T(8,128)(2,1)S(1)}, bf16[32,128,128]{2,1,0:T(8,128)(2,1)}, u32[]{:S(2)}) copy-start(bf16[32,128,128]{2,1,0:T(8,128)(2,1)} %wg_hbm.1) | copy-start | bytes 3145732
  4.5 1.2 %copy-start.2 = (bf16[32,128,128]{2,1,0:T(8,128)(2,1)S(1)}, bf16[32,128,128]{2,1,0:T(8,128)(2,1)}, u32[]{:S(2)}) copy-start(bf16[32,128,128]{2,1,0:T(8,128)(2,1)} %wd_hbm.1) | copy-start | bytes 3145732
  5.7 0.8 %copy-start.3 = (bf16[2,8192]{1,0:T(2,128)(2,1)S(1)}, bf16[2,8192]{1,0:T(2,128)(2,1)}, u32[]{:S(2)}) copy-start(bf16[2,8192]{1,0:T(2,128)(2,1)} %tok_ref.1) | copy-start | bytes 98308
  6.5 0.8 %copy-start.4 = (bf16[2,8192]{1,0:T(2,128)(2,1)S(1)}, bf16[2,8192]{1,0:T(2,128)(2,1)}, u32[]{:S(2)}) copy-start(bf16[2,8192]{1,0:T(2,128)(2,1)} %cot_ref.1) | copy-start | bytes 98308

commit v2 on v1

--- a/solution.py
+++ b/solution.py
@@ -19,10 +19,10 @@
 
 
 def layer_kernel(
-    n, lay_ref, cnt_ref, tok_ref, cot_ref, wu_hbm, wg_hbm, wd_hbm,
-    xg, yg, hid, dup, dgt, outp, dxp,
-    wu, wg, wd, mx, terms, terms2, inv_v, inv_s, po, own, r1, t2, r2, t3, r3,
-    wsem, isem, gsend, grecv, s1, q1, lsem, s2, q2, s3, q3,
+    n, lu_hbm, lg_hbm, ld_hbm, cnt_hbm, tok_hbm, cot_hbm, wu_hbm, wg_hbm, wd_hbm,
+    xg_hbm, yg_hbm, hid_hbm, dup_hbm, dgt_hbm, outp, dxp,
+    xg, yg, hid, dup, dgt, lay_ref, cnt_ref, tok_ref, cot_ref, wu, wg, wd, mx, terms, terms2, inv_v, inv_s, po, own, r1, t2, r2, t3, r3,
+    osem, asem, wsem, isem, gsend, grecv, s1, q1, lsem, s2, q2, s3, q3,
 ):
     nz = n // 4
     db = xg.shape[0]
@@ -42,6 +42,15 @@
     def dev(j):
         return {"tensor": j}
 
+    acopies = [
+        pltpu.make_async_copy(src, dst, asem.at[i])
+        for i, (src, dst) in enumerate((
+            (tok_hbm, tok_ref), (cot_hbm, cot_ref), (cnt_hbm, cnt_ref),
+            (lu_hbm, lay_ref.at[0]), (lg_hbm, lay_ref.at[1]), (ld_hbm, lay_ref.at[2]),
+        ))
+    ]
+    for c in acopies:
+        c.start()
     wcopies = [
         pltpu.make_async_copy(src, dst, wsem.at[i])
         for i, (src, dst) in enumerate(((wu_hbm, wu), (wg_hbm, wg), (wd_hbm, wd)))
@@ -55,6 +64,8 @@
             barrier, inc=1, device_id=dev(j), device_id_type=pl.DeviceIdType.MESH
         )
 
+    for c in acopies[:2]:
+        c.wait()
     for c in range(db):
         xg[c, me] = tok_ref[:, c * bs:(c + 1) * bs]
         yg[c, me] = cot_ref[:, c * bs:(c + 1) * bs]
@@ -94,11 +105,13 @@
         gsendto(a, me, pair)
         gsendto(a, me, sib)
 
+    for c in acopies[2:]:
+        c.wait()
     lane = lax.broadcasted_iota(jnp.int32, (8, 256), 1)
     for m in range(3):
         tab = jnp.full((8, 256), slots, jnp.int32)
         for s in range(slots):
-            code = jnp.where(s < cnt_ref[m, 0], lay_ref[m, s], -1)
+            code = jnp.where(s < cnt_ref[m], lay_ref[m, s], -1)
             tab = jnp.where(lane == code, s, tab)
         inv_v[m] = tab
     icopy = pltpu.make_async_copy(inv_v, inv_s, isem.at[0])
@@ -128,7 +141,7 @@
         def pick(s, carry):
             code = lay_ref[m, s]
             major = third(code)
-            minor = jnp.where(s < cnt_ref[m, 0], code - 3 * major, HB)
+            minor = jnp.where(s < cnt_ref[m], code - 3 * major, HB)
             rows_s = view[major]
             for h in range(HB):
                 mx[s, h * tt:(h + 1) * tt, :] = jnp.where(
@@ -235,10 +248,17 @@
                 src[minor], weights[s], dims, preferred_element_type=F32
             )
 
+    ocopies = [
+        pltpu.make_async_copy(src, dst, osem.at[i])
+        for i, (src, dst) in enumerate((
+            (xg, xg_hbm), (yg, yg_hbm), (hid, hid_hbm), (dup, dup_hbm), (dgt, dgt_hbm)
+        ))
+    ]
     forward_z(0)
     forward_y(0)
     forward_z(1)
     finish(0)
+    ocopies[0].start()
     wcopies[0].wait()
     up = contract(xg, 0, wu, False)
     wcopies[1].wait()
@@ -246,6 +266,7 @@
     sig = 1.0 / (1.0 + jnp.exp(-gate))
     act = gate * sig
     hid.reshape(HB * tt, bs)[...] = (act * up).astype(BF16)
+    ocopies[2].start()
     forward_y(1)
     wcopies[2].wait()
     icopy.wait()
@@ -253,11 +274,14 @@
     scatter(0, ((2, terms),))
     reduce_core(0)
     finish(1)
+    ocopies[1].start()
     d_hidden = contract(yg, 2, wd, True)
     dup.reshape(HB * tt, bs)[...] = (d_hidden * act).astype(BF16)
     dgt.reshape(HB * tt, bs)[...] = (
         d_hidden * up * sig * (1.0 + gate * (1.0 - sig))
     ).astype(BF16)
+    ocopies[3].start()
+    ocopies[4].start()
     reduce_pair(0)
     expand(wu, dup, 0, terms, NT)
     expand(wg, dgt, 1, terms2, NT)
@@ -270,10 +294,12 @@
     reduce_end(1, total1, dxp)
     for c in pending:
         c.wait_send()
+    for c in ocopies:
+        c.wait()
 
 
 def grads_kernel(
-    per, lay_ref, cnt_ref, xg, yg, hid, dup, dgt, outp, dxp,
+    per, lu_ref, lg_ref, ld_ref, cnt_ref, xg, yg, hid, dup, dgt, outp, dxp,
     out, dx, gu, gg, gd,
 ):
     step = pl.program_id(0)
@@ -287,15 +313,15 @@
 
     for i in range(per):
         s = step * per + i
-        for m, grad in ((0, gu), (1, gg), (2, gd)):
-            code = lay_ref[m, s]
+        for m, lay, grad in ((0, lu_ref, gu), (1, lg_ref, gg), (2, ld_ref, gd)):
+            code = lay[s]
             major = third(code)
             minor = code - 3 * major
             if m == 2:
                 lhs, rhs = hid[minor], yg[major]
             else:
                 lhs, rhs = xg[major], (dup, dgt)[m][minor]
-            lhs = jnp.where(s < cnt_ref[m, 0], lhs, jnp.zeros_like(lhs))
+            lhs = jnp.where(s < cnt_ref[m], lhs, jnp.zeros_like(lhs))
             grad[i] = lax.dot_general(
                 lhs, rhs, TN, preferred_element_type=F32
             ).astype(BF16)
@@ -305,10 +331,10 @@
     rows, width = tokens.shape
     slots, bs, _ = wu.shape
     db, tt, nz = width // bs, n * rows, n // 4
-    layout = jnp.stack([lu, lg, ld])
+    counts = counts.reshape(3)
     vm = pl.BlockSpec(memory_space=pltpu.VMEM)
     sm = pl.BlockSpec(memory_space=pltpu.SMEM)
-    hbm = pl.BlockSpec(memory_space=pl.ANY)
+    hbm = pl.BlockSpec(memory_space=pltpu.HBM)
     shape = jax.ShapeDtypeStruct
     dma = pltpu.SemaphoreType.DMA
     part = (nz, db, rows, bs)
@@ -317,9 +343,18 @@
         out_shape=[shape((db, n, rows, bs), BF16)] * 2
         + [shape((HB, tt, bs), BF16)] * 3
         + [shape((db, rows, bs), BF16)] * 2,
-        in_specs=[sm, sm, vm, vm, hbm, hbm, hbm],
-        out_specs=[vm] * 7,
+        in_specs=[hbm] * 9,
+        out_specs=[hbm] * 5 + [vm] * 2,
         scratch_shapes=[
+            pltpu.VMEM((db, n, rows, bs), BF16),
+            pltpu.VMEM((db, n, rows, bs), BF16),
+            pltpu.VMEM((HB, tt, bs), BF16),
+            pltpu.VMEM((HB, tt, bs), BF16),
+            pltpu.VMEM((HB, tt, bs), BF16),
+            pltpu.SMEM((3, slots), jnp.int32),
+            pltpu.SMEM((3,), jnp.int32),
+            pltpu.VMEM((rows, width), BF16),
+            pltpu.VMEM((rows, width), BF16),
             pltpu.VMEM((slots, bs, bs), BF16),
             pltpu.VMEM((slots, bs, bs), BF16),
             pltpu.VMEM((slots, bs, bs), BF16),
@@ -335,15 +370,15 @@
             pltpu.VMEM((2,) + part, BF16),
             pltpu.VMEM((2,) + part, BF16),
             pltpu.VMEM((2,) + part, BF16),
-            dma((3,)), dma((1,)), dma((2, n)), dma((2, n)),
+            dma((5,)), dma((6,)), dma((3,)), dma((1,)), dma((2, n)), dma((2, n)),
             dma((2, nz, 2)), dma((2, nz, 2)), dma((2, nz, 2)),
             dma((2, nz)), dma((2, nz)), dma((2, nz)), dma((2, nz)),
         ],
         compiler_params=pltpu.CompilerParams(
-            collective_id=0, has_side_effects=True, vmem_limit_bytes=48 << 20
+            collective_id=0, has_side_effects=True, vmem_limit_bytes=64 << 20
         ),
         name="layer",
-    )(layout, counts, tokens, cotangent, wu, wg, wd)
+    )(lu, lg, ld, counts, tokens, cotangent, wu, wg, wd)
     xg = xg.reshape(db, tt, bs)
     yg = yg.reshape(db, tt, bs)
     per = slots // 4
@@ -358,11 +393,11 @@
         functools.partial(grads_kernel, per),
         grid=(4,),
         out_shape=[shape((rows, width), BF16)] * 2 + [shape((slots, bs, bs), BF16)] * 3,
-        in_specs=[sm, sm] + [whole(a) for a in rest],
+        in_specs=[sm] * 4 + [whole(a) for a in rest],
         out_specs=[row, row, block, block, block],
-        compiler_params=pltpu.CompilerParams(vmem_limit_bytes=48 << 20),
+        compiler_params=pltpu.CompilerParams(vmem_limit_bytes=64 << 20),
         name="grads",
-    )(layout, counts, *rest)
+    )(lu, lg, ld, counts, *rest)
 
 
 def solution(mesh):

time: 46.8 us -> 40.6 us (0.87)
  local copies, waits for them, and re-layouts: 6.59 us -> 0 us
  Pallas kernels: 39.1 us -> 39.8 us
    unnamed x19 -> x0, local copies, waits for them, and re-layouts: 6.59 us -> none
    pallas_call x1, Pallas kernels: 3.63 us -> 4.35 us  [local_part(): pl.pallas_call(functools.partial(grads_kernel, per), grid=(4,), out_shape...]
where the time goes in v2:
time: 40.6 us; the launch traced here: 40.4 us
  Pallas kernels  39.8 us (98%)
  between operations  0.64 us (2%)
    pallas_call x1, Pallas kernels, local_part(): pl.pallas_call(functools.partial(layer_kernel, n), out_shape=[shape((db,...  35.4 us
    pallas_call x1, Pallas kernels, local_part(): pl.pallas_call(functools.partial(grads_kernel, per), grid=(4,), out_shape...  4.35 us

profile of v2, /device:TPU:0, one launch (start us, length us, event | category | flops | bytes accessed | tf_op | source)
XLA Modules:
  0.0 40.4 jit_solution(2195502018964035385)
XLA Ops:
  0.6 35.4 %layer.1 = (bf16[64,16,2,128]{3,2,1,0:T(2,128)(2,1)}, bf16[64,16,2,128]{3,2,1,0:T(2,128)(2,1)}, bf16[3,32,128]{2,1,0:T(8,128)(2,1)}, bf16[3,32,128]{2,1,0:T(8,12...) custom-call(s32[32]{0:T(128)} %lu_ref.1, s32[32]{0:T(128)} %lg_ref.1, ...), custom_call_target="tpu_custom_call" | custom-call | tf_op jit(solution)/shard_map/layer/pallas_call | solution.py:341
  36.1 4.3 %grads.1 = (bf16[2,8192]{1,0:T(2,128)(2,1)}, bf16[2,8192]{1,0:T(2,128)(2,1)}, bf16[32,128,128]{2,1,0:T(8,128)(2,1)}, bf16[32,128,128]{2,1,0:T(8,128)(2,1)}, bf16[32,128,128]{2,1,0:T(8,128)(2,1)}) custom-call(s32[32]{0:T(128)} %lu_ref.1, s32[32]{0:T(128)} %lg_ref.1, s32[32]{0:T(128)} %ld_ref.1, s32[3]{0:T(128)} %bitcast.6, bf16[64,32,128]{2,1,0:T(8,128)(2,1)} %bitcast.3, ...), custom_call_target="tpu_custom_call" | custom-call | tf_op jit(solution)/shard_map/grads/pallas_call | solution.py:392

commit v3 on v2

--- a/solution.py
+++ b/solution.py
@@ -34,7 +34,15 @@
     z, y, p = me // 4, (me // 2) % 2, me % 2
     sib = me + 1 - 2 * p
     pair = me + 2 - 4 * y
-    zs = [(z + k) % nz for k in range(nz)]
+    low = jnp.minimum(z, nz - 1 - z)
+
+    def ranked(k):
+        half = (k + 1) // 2
+        beside = z + half if k % 2 else z - half
+        beyond = jnp.where(2 * z < nz, z + (k - low), z - (k - low))
+        return jnp.where(k <= 2 * low, beside, beyond)
+
+    zs = [z] + [ranked(k) for k in range(1, nz)]
 
     def at(zz, yy, pp):
         return zz * 4 + yy * 2 + pp
@@ -100,7 +108,7 @@
         ).wait_recv()
 
     for a in range(2):
-        for zz in zs[1:]:
+        for zz in zs[:0:-1]:
             gsendto(a, me, at(zz, y, p))
         gsendto(a, me, pair)
         gsendto(a, me, sib)
@@ -172,7 +180,7 @@
         lax.fori_loop(0, db, place, 0, unroll=4)
 
     flat = (db * rows, bs)
-    order = zs[1:] + zs[:1]
+    order = zs[::-1]
 
     def remote(src, dst, send, recv, j):
         return pltpu.make_async_remote_copy(
@@ -211,23 +219,21 @@
     def store(ref, value, *idx):
         ref.at[idx].reshape(*flat)[...] = value.astype(BF16)
 
-    def reduce_pair(a):
-        for zz in order:
-            copy1(a, zz, 1 - y).wait_recv()
-            local(a, zz, 1 - y).wait()
-            store(t2, load(own, a, zz, 1 - y) + load(r1, a, zz, 1 - y), a, zz)
-            copy2(a, zz).start()
-
-    def reduce_z(a):
-        for zz in order:
-            copy1(a, zz, y).wait_recv()
-            local(a, zz, y).wait()
-            copy2(a, zz).wait_recv()
-            total = load(own, a, zz, y) + load(r1, a, zz, y) + load(r2, a, zz)
-            if zz is zs[0]:
-                return total
+    def pair_step(a, zz):
+        copy1(a, zz, 1 - y).wait_recv()
+        local(a, zz, 1 - y).wait()
+        store(t2, load(own, a, zz, 1 - y) + load(r1, a, zz, 1 - y), a, zz)
+        copy2(a, zz).start()
+
+    def z_step(a, zz):
+        copy1(a, zz, y).wait_recv()
+        local(a, zz, y).wait()
+        copy2(a, zz).wait_recv()
+        total = load(own, a, zz, y) + load(r1, a, zz, y) + load(r2, a, zz)
+        if zz is not zs[0]:
             store(t3, total, a, zz)
             copy3(a, zz, z).start()
+        return total
 
     def reduce_end(a, total, result):
         for zz in zs[1:]:
@@ -255,8 +261,8 @@
         ))
     ]
     forward_z(0)
+    forward_z(1)
     forward_y(0)
-    forward_z(1)
     finish(0)
     ocopies[0].start()
     wcopies[0].wait()
@@ -282,14 +288,17 @@
     ).astype(BF16)
     ocopies[3].start()
     ocopies[4].start()
-    reduce_pair(0)
+    for zz in order:
+        pair_step(0, zz)
     expand(wu, dup, 0, terms, NT)
     expand(wg, dgt, 1, terms2, NT)
     scatter(1, ((0, terms), (1, terms2)))
     reduce_core(1)
-    total0 = reduce_z(0)
-    reduce_pair(1)
-    total1 = reduce_z(1)
+    for zz in order:
+        total0 = z_step(0, zz)
+        pair_step(1, zz)
+    for zz in order:
+        total1 = z_step(1, zz)
     reduce_end(0, total0, outp)
     reduce_end(1, total1, dxp)
     for c in pending:

time: 40.6 us -> 38.2 us (0.941)
  Pallas kernels: 39.8 us -> 37.4 us
    pallas_call x1, Pallas kernels: 35.4 us -> 33.1 us  [local_part(): pl.pallas_call(functools.partial(layer_kernel, n), out_shape=[shape((db,...]
where the time goes in v3:
time: 38.2 us; the launch traced here: 38.1 us
  Pallas kernels  37.4 us (98%)
  between operations  0.64 us (2%)
    pallas_call x1, Pallas kernels, local_part(): pl.pallas_call(functools.partial(layer_kernel, n), out_shape=[shape((db,...  33.1 us
    pallas_call x1, Pallas kernels, local_part(): pl.pallas_call(functools.partial(grads_kernel, per), grid=(4,), out_shape...  4.35 us

profile of v3, /device:TPU:0, one launch (start us, length us, event | category | flops | bytes accessed | tf_op | source)
XLA Modules:
  0.0 38.1 jit_solution(6249332467926922076)
XLA Ops:
  0.6 33.1 %layer.1 = (bf16[64,16,2,128]{3,2,1,0:T(2,128)(2,1)}, bf16[64,16,2,128]{3,2,1,0:T(2,128)(2,1)}, bf16[3,32,128]{2,1,0:T(8,128)(2,1)}, bf16[3,32,128]{2,1,0:T(8,12...) custom-call(s32[32]{0:T(128)} %lu_ref.1, s32[32]{0:T(128)} %lg_ref.1, ...), custom_call_target="tpu_custom_call" | custom-call | tf_op jit(solution)/shard_map/layer/pallas_call | solution.py:350
  33.7 4.3 %grads.1 = (bf16[2,8192]{1,0:T(2,128)(2,1)}, bf16[2,8192]{1,0:T(2,128)(2,1)}, bf16[32,128,128]{2,1,0:T(8,128)(2,1)}, bf16[32,128,128]{2,1,0:T(8,128)(2,1)}, bf16[32,128,128]{2,1,0:T(8,128)(2,1)}) custom-call(s32[32]{0:T(128)} %lu_ref.1, s32[32]{0:T(128)} %lg_ref.1, s32[32]{0:T(128)} %ld_ref.1, s32[3]{0:T(128)} %bitcast.6, bf16[64,32,128]{2,1,0:T(8,128)(2,1)} %bitcast.3, ...), custom_call_target="tpu_custom_call" | custom-call | tf_op jit(solution)/shard_map/grads/pallas_call | solution.py:401
